TPU v7x, 32 devices: a whole 2x2x4 slice. The times are simulated.
32 devices in a mesh: wall: 4 (over z), stream: 8 (over y, x, core).
Axes of the slice: x: 2, y: 2, z: 4, core: 2. Of those that a mesh axis runs over, the one named last changes fastest.
Arguments:
- state: float32 [20, 135, 2048], P('wall', None, 'stream'), may hold values from -6 to 6
- pivot_inv: float32 [20, 135, 135], P('wall'), may hold values from -0.02 to 0.2
- lower_block: float32 [20, 135, 135], P('wall'), may hold values from -22 to 1.5
- upper_block: float32 [20, 135, 135], P('wall'), may hold values from -1.2 to 0.2
- volume: float32 [135, 135], replicated, may hold values from -0.5 to 0.5
- face_minus: float32 [45, 135], replicated, may hold values from -0.5 to 0.5
- face_plus: float32 [45, 135], replicated, may hold values from -0.5 to 0.5
- lift_minus: float32 [135, 45], replicated, may hold values from -0.875 to 0.875
- lift_plus: float32 [135, 45], replicated, may hold values from -0.875 to 0.875
- offsets: int32 [2048], P('stream'), may hold values from 0 to 4
- counts: int32 [2048], P('stream'), may hold values from 10 to 15
Outputs:
- section_state: float32 [20, 135, 2048], P('wall', None, 'stream')
- section_rate: float32 [20, 135, 2048], P('wall', None, 'stream')
All inputs are finite; a program needn't handle non-finite values.
Results may differ from a plain program's by a relative error of at most 0.00019.
Values sent between devices are 32-bit elements; how exact they have to be, the bound alone decides.
A program may use at most 64 MiB of HBM per device.

v0:
```python
import jax
import jax.numpy as jnp
from jax import lax
from jax.sharding import PartitionSpec as P

section_step = 0.4


def padded(cells, sides, width):
    for axis, dim in sides:
        count = lax.axis_size(axis)
        head = lax.slice_in_dim(cells, 0, width, axis=dim)
        tail = lax.slice_in_dim(cells, cells.shape[dim] - width, cells.shape[dim], axis=dim)
        cells = jnp.concatenate(
            [
                lax.ppermute(tail, axis, [(i, (i + 1) % count) for i in range(count)]),
                cells,
                lax.ppermute(head, axis, [((i + 1) % count, i) for i in range(count)]),
            ],
            axis=dim,
        )
    return cells


def product(left, right):
    return jnp.dot(left, right, precision=lax.Precision.HIGHEST)


def batched(matrix, field):
    return jnp.einsum("fb,kbl->kfl", matrix, field, precision=lax.Precision.HIGHEST)


def explicit_rate(field, volume, face_minus, face_plus, lift_minus, lift_plus):
    traces = jnp.stack((batched(face_minus, field), batched(face_plus, field)))
    widened = padded(traces, (("stream", 3),), 1)
    minus_next = widened[0, :, :, 2:]
    plus_prev = widened[1, :, :, :-2]
    jump_upper = minus_next - traces[1]
    jump_lower = traces[0] - plus_prev
    return batched(volume, field) + batched(lift_plus, jump_upper) + batched(lift_minus, jump_lower)


def ordered_prefix(maps_all, rows_all, position, backwards):
    total = maps_all.shape[0]

    def advance(turn, carry):
        source = total - 1 - turn if backwards else turn
        taken = source > position if backwards else source < position
        map_now = lax.dynamic_index_in_dim(maps_all, source, 0, keepdims=False)
        rows_now = lax.dynamic_index_in_dim(rows_all, source, 0, keepdims=False)
        moved = product(map_now, carry) + rows_now
        return jnp.where(taken, moved, carry)

    return lax.fori_loop(0, total, advance, jnp.zeros_like(rows_all[0]))


def body(
    state,
    pivot_inv,
    lower_block,
    upper_block,
    volume,
    face_minus,
    face_plus,
    lift_minus,
    lift_plus,
    offsets,
    counts,
):
    elements = state.shape[0]
    position = lax.axis_index("wall")
    element = position * elements + jnp.arange(elements, dtype=jnp.int32)
    ending = offsets + counts
    active = ((offsets[None, :] <= element[:, None]) & (element[:, None] < ending[None, :])).astype(
        jnp.float32
    )[:, None, :]
    rate = explicit_rate(state, volume, face_minus, face_plus, lift_minus, lift_plus)
    right_side = active * (state + section_step * rate)
    local_rows = []
    spikes = []
    for index in range(elements):
        if index == 0:
            current = product(pivot_inv[0], right_side[0])
            spike_term = -product(pivot_inv[0], lower_block[0])
        else:
            current = product(
                pivot_inv[index], right_side[index] - product(lower_block[index], current)
            )
            spike_term = -product(pivot_inv[index], product(lower_block[index], spike_term))
        local_rows.append(current)
        spikes.append(spike_term)
    maps_all, rows_all = (
        lax.all_gather(spikes[-1][None], "wall", axis=0, tiled=True),
        lax.all_gather(local_rows[-1][None], "wall", axis=0, tiled=True),
    )
    entering = ordered_prefix(maps_all, rows_all, position, False)
    forward_rows = [
        local_rows[index] + product(spikes[index], entering) for index in range(elements)
    ]
    back_rows = [None] * elements
    reach_map = [None] * elements
    for index in reversed(range(elements)):
        if index == elements - 1:
            back_rows[index] = forward_rows[index]
            reach_map[index] = -upper_block[index]
        else:
            back_rows[index] = forward_rows[index] - product(
                upper_block[index], back_rows[index + 1]
            )
            reach_map[index] = -product(upper_block[index], reach_map[index + 1])
    maps_up, rows_up = (
        lax.all_gather(reach_map[0][None], "wall", axis=0, tiled=True),
        lax.all_gather(back_rows[0][None], "wall", axis=0, tiled=True),
    )
    above = ordered_prefix(maps_up, rows_up, position, True)
    solution = jnp.stack(
        [back_rows[index] + product(reach_map[index], above) for index in range(elements)]
    )
    section_state = active * solution
    section_rate = active * explicit_rate(
        section_state, volume, face_minus, face_plus, lift_minus, lift_plus
    )
    return (section_state, section_rate)


def solution(mesh):
    in_specs = (
        P("wall", None, "stream"),
        P("wall", None, None),
        P("wall", None, None),
        P("wall", None, None),
        P(),
        P(),
        P(),
        P(),
        P(),
        P("stream"),
        P("stream"),
    )
    out_specs = (P("wall", None, "stream"), P("wall", None, "stream"))
    return jax.shard_map(body, mesh=mesh, in_specs=in_specs, out_specs=out_specs, check_vma=False)
```

profile of v0, /device:TPU:1, one launch (start us, length us, event | category | flops | bytes accessed | tf_op | source)
XLA Modules:
  0.0 113.6 jit_solution(6355811358400327991)
XLA Ops:
  0.7 1.7 %fusion.142 = f32[5,256,45]{1,2,0:T(8,128)S(1)} fusion(f32[5,135,256]{2,1,0:T(8,128)} %param.15, f32[45,135]{1,0:T(8,128)} %param.20), kind=kOutput, calls=%fused_computation.192 | convolution fusion | flops 93312000 | bytes 945900 | tf_op jit(solution)/shard_map/fb,kbl->kfl/dot_general | solution.py:30
  2.4 0.5 fusion.138
  2.9 0.8 pad_maximum_fusion.10
  3.8 2.6 %collective-permute-start.1 = (f32[2,5,45,1]{3,2,1,0:T(8,128)}, f32[2,5,45,1]{3,2,1,0:T(8,128)}, u32[]{:S(2)}, u32[]{:S(2)}) collective-permute-start(f32[2,5,45,1]{3,2,1,0:T(8,128)} %get-tuple-element.298), channel_id=1, source_target_pairs={{0,1},{1,2},{2,3},{3,4},{4,5},{5,6},{6,7},{7,0},{8,9},{9,10},{10,1... | collective-permute-start | bytes 5408 | tf_op jit(solution)/shard_map/ppermute | solution.py:16
  6.4 1.6 %fusion.103 = f32[5,256,135]{1,2,0:T(8,128)} fusion(f32[5,135,256]{2,1,0:T(8,128)S(1)} %copy-done.1, f32[135,135]{1,0:T(8,128)S(1)} %copy-done), kind=kOutput, calls=%fused_computation.152 | convolution fusion | flops 279936000 | bytes 1455300 | tf_op jit(solution)/shard_map/fb,kbl->kfl/dot_general | solution.py:30
  8.0 0.6 iota_add_fusion
  12.8 0.5 copy-done.21
  13.3 14.7 %all-gather.4 = f32[4,135,135]{2,1,0:T(8,128)S(1)} all-gather(f32[1,135,135]{2,1,0:T(8,128)S(1)} %copy.15), channel_id=2, replica_groups=mesh['wall'=4,'stream'=8] {'wall'}, dimensions={0}, use_global_device_ids=true | all-gather | bytes 364500 | tf_op jit(solution)/shard_map/all_gather | solution.py:93
  28.3 0.5 convolution_negate_fusion.2
  29.4 0.9 convolution_negate_fusion
  30.4 1.0 copy.16
  31.5 0.7 copy-done.41
  32.1 0.7 and_convert_fusion
  32.8 12.0 %all-gather.6 = f32[4,135,135]{2,1,0:T(8,128)S(1)} all-gather(f32[1,135,135]{2,1,0:T(8,128)S(1)} %copy.16), channel_id=4, replica_groups=mesh['wall'=4,'stream'=8] {'wall'}, dimensions={0}, use_global_device_ids=true | all-gather | bytes 364500 | tf_op jit(solution)/shard_map/all_gather | solution.py:112
  44.8 2.1 %convolution_add_fusion.5 = f32[5,256,135]{1,2,0:T(8,128)S(1)} fusion(f32[5,256,135]{1,2,0:T(8,128)} %fusion.103, f32[2,5,45,1]{3,2,1,0:T(8,128)} %collective-permute-done, f32[1,5,45,256]{3,2,1,0:T(8,128)S(1)} %bitcast.322, f32[1,5,45,256]{3,2,1,0:T(8,128)S(1)} %bitcast.319, f32[5,256,45]{1,2,0:T(8,128)S(1)} %fusion.138, f32[135,45]{0,1:T(8,128)} %param.23), kind=kOutput, calls=%fused_computation.27 | convolution fusion | flops 93657600 | bytes 2099700 | tf_op jit(solution)/shard_map/fb,kbl->kfl/dot_general | solution.py:30
  46.9 1.8 %fusion.21 = f32[5,135,256]{2,1,0:T(8,128)S(1)} fusion(f32[5,135,256]{2,1,0:T(8,128)S(1)} %copy-done.1, f32[5,256,135]{1,2,0:T(8,128)S(1)} %convolution_add_fusion.5, f32[5,256]{1,0:T(8,128)S(1)} %copy-done.37, f32[2,5,45,1]{3,2,1,0:T(8,128)} %collective-permute-done.1, f32[1,5,45,256]{3,2,1,0:T(8,128)S(1)} %bitcast.323, ...), kind=kOutput, calls=%fused_computation.26 | convolution fusion | flops 94176000 | bytes 2796020 | tf_op jit(solution)/shard_map/fb,kbl->kfl/dot_general | solution.py:30
  52.4 12.8 %all-gather.5 = f32[4,135,256]{2,1,0:T(8,128)S(1)} all-gather(f32[1,135,256]{2,1,0:T(8,128)S(1)} %bitcast.333), channel_id=3, replica_groups=mesh['wall'=4,'stream'=8] {'wall'}, dimensions={0}, use_global_device_ids=true | all-gather | bytes 691200 | tf_op jit(solution)/shard_map/all_gather | solution.py:94
  65.2 1.3 %while.30 = (s32[]{:T(128)}, f32[135,256]{1,0:T(8,128)S(1)}, s32[]{:T(128)}, f32[4,135,135]{2,1,0:T(8,128)S(1)}, f32[4,135,256]{2,1,0:T(8,128)S(1)}, /*index=5*/s32[]{:T(128)}, s32[]{:T(128)}) while((s32[]{:T(128)}, f32[135,256]{1,0:T(8,128)S(1)}, s32[]{:T(128)}, f32[4,135,135]{2,1,0:T(8,128)S(1)}, f32[4,135,256]{2,1,0:T(8,128)S(1)}, ...), condition=%wide.region_1.2_spmd.clone, body=%wide.region_0.1_spmd.clone.sunk | while | flops 56125444 | bytes 974431 | solution.py:54
  67.6 0.5 convolution_add_fusion.11
  71.4 12.0 %all-gather.7 = f32[4,135,256]{2,1,0:T(8,128)S(1)} all-gather(f32[1,135,256]{2,1,0:T(8,128)S(1)} %bitcast.332), channel_id=5, replica_groups=mesh['wall'=4,'stream'=8] {'wall'}, dimensions={0}, use_global_device_ids=true | all-gather | bytes 691200 | tf_op jit(solution)/shard_map/all_gather | solution.py:113
  83.4 1.3 %while.31 = (s32[]{:T(128)}, f32[135,256]{1,0:T(8,128)S(1)}, s32[]{:T(128)}, f32[4,135,135]{2,1,0:T(8,128)S(1)}, f32[4,135,256]{2,1,0:T(8,128)S(1)}, /*index=5*/s32[]{:T(128)}, s32[]{:T(128)}, s32[]{:T(128)}, s32[]{:T(128)}) while((s32[]{:T(128)}, f32[135,256]{1,0:T(8,128)S(1)}, s32[]{:T(128)}, f32[4,135,135]{2,1,0:T(8,128)S(1)}, ...), condition=%wide.region_3.4_spmd.clone, body=%wide.region_2.3_spmd.clone.sunk | while | flops 56125448 | bytes 974493 | solution.py:54
  85.6 0.5 fusion.38
  86.5 0.5 fusion.36
  88.0 0.7 copy-done.31
  88.8 0.5 fusion.140
  89.6 0.5 fusion.136
  90.3 12.2 %collective-permute-start.2 = (f32[2,5,45,1]{3,2,1,0:T(8,128)S(1)}, f32[2,5,45,1]{3,2,1,0:T(8,128)S(1)}, u32[]{:S(2)}, u32[]{:S(2)}) collective-permute-start(f32[2,5,45,1]{3,2,1,0:T(8,128)S(1)} %get-tuple-element.297), channel_id=1, source_target_pairs={{1,0},{2,1},{3,2},{4,3},{5,4},{6,5},{7,6},{0,7},{9,8},{10,9},{11,1... | collective-permute-start | bytes 5408 | tf_op jit(solution)/shard_map/ppermute | solution.py:18
  102.5 0.7 fusion.101
  103.2 2.4 %collective-permute-start.3 = (f32[2,5,45,1]{3,2,1,0:T(8,128)S(1)}, f32[2,5,45,1]{3,2,1,0:T(8,128)S(1)}, u32[]{:S(2)}, u32[]{:S(2)}) collective-permute-start(f32[2,5,45,1]{3,2,1,0:T(8,128)S(1)} %get-tuple-element.296), channel_id=1, source_target_pairs={{0,1},{1,2},{2,3},{3,4},{4,5},{5,6},{6,7},{7,0},{8,9},{9,10},{10,1... | collective-permute-start | bytes 5408 | tf_op jit(solution)/shard_map/ppermute | solution.py:16
  105.6 5.3 %collective-permute-done.2 = f32[2,5,45,1]{3,2,1,0:T(8,128)S(1)} collective-permute-done((f32[2,5,45,1]{3,2,1,0:T(8,128)S(1)}, f32[2,5,45,1]{3,2,1,0:T(8,128)S(1)}, u32[]{:S(2)}, u32[]{:S(2)}) %collective-permute-start.2) | collective-permute-done | bytes 1832 | tf_op jit(solution)/shard_map/ppermute | solution.py:18
  111.0 0.9 convolution_add_fusion.3
  111.9 1.7 %fusion.17 = f32[5,135,256]{2,1,0:T(8,128)} fusion(f32[5,256,135]{1,2,0:T(8,128)S(1)} %convolution_add_fusion.3, f32[5,256]{1,0:T(8,128)S(1)} %copy-done.38, f32[2,5,45,1]{3,2,1,0:T(8,128)S(1)} %collective-permute-done.3, f32[1,5,45,256]{3,2,1,0:T(8,128)S(1)} %bitcast.329, f32[1,5,45,256]{3,2,1,0:T(8,128)S(1)} %bitcast.326, f32[5,256,45]{1,2,0:T(8,128)S(1)} %fusion.140, ...), kind=kOutput, calls=%fused_computation.20 | convolution fusion | flops 93830400 | bytes 2104820 | tf_op jit(solution)/shard_map/fb,kbl->kfl/dot_general | solution.py:30
  (138 shorter events, 17.9 us)
Async XLA Ops:
  0.6 5.7 %copy-start = (f32[135,135]{1,0:T(8,128)S(1)}, f32[135,135]{1,0:T(8,128)}, u32[]{:S(2)}) copy-start(f32[135,135]{1,0:T(8,128)} %param.19) | copy-start | bytes 218704
  0.6 1.7 %copy-start.1 = (f32[5,135,256]{2,1,0:T(8,128)S(1)}, f32[5,135,256]{2,1,0:T(8,128)}, u32[]{:S(2)}) copy-start(f32[5,135,256]{2,1,0:T(8,128)} %param.15) | copy-start | bytes 2073604
  0.7 1.7 %copy-start.32 = (f32[45,135]{1,0:T(8,128)S(1)}, f32[45,135]{1,0:T(8,128)}, u32[]{:S(2)}) copy-start(f32[45,135]{1,0:T(8,128)} %param.21) | copy-start | bytes 72904
  3.8 41.0 %collective-permute-start = (f32[2,5,45,1]{3,2,1,0:T(8,128)}, f32[2,5,45,1]{3,2,1,0:T(8,128)}, u32[]{:S(2)}, u32[]{:S(2)}) collective-permute-start(f32[2,5,45,1]{3,2,1,0:T(8,128)} %get-tuple-element.299), channel_id=1, source_target_pairs={{1,0},{2,1},{3,2},{4,3},{5,4},{6,5},{7,6},{0,7},{9,8},{10,9},{11,1... | collective-permute-start | bytes 5408 | tf_op jit(solution)/shard_map/ppermute | solution.py:18
  3.8 43.1 %collective-permute-start.1 = (f32[2,5,45,1]{3,2,1,0:T(8,128)}, f32[2,5,45,1]{3,2,1,0:T(8,128)}, u32[]{:S(2)}, u32[]{:S(2)}) collective-permute-start(f32[2,5,45,1]{3,2,1,0:T(8,128)} %get-tuple-element.298), channel_id=1, source_target_pairs={{0,1},{1,2},{2,3},{3,4},{4,5},{5,6},{6,7},{7,0},{8,9},{9,10},{10,1... | collective-permute-start | bytes 5408 | tf_op jit(solution)/shard_map/ppermute | solution.py:16
  6.4 2.2 %copy-start.3 = (f32[5,135,135]{2,1,0:T(8,128)S(1)}, f32[5,135,135]{2,1,0:T(8,128)}, u32[]{:S(2)}) copy-start(f32[5,135,135]{2,1,0:T(8,128)} %param.16) | copy-start | bytes 1093504
  6.4 2.2 %copy-start.6 = (f32[5,135,135]{2,1,0:T(8,128)S(1)}, f32[5,135,135]{2,1,0:T(8,128)}, u32[]{:S(2)}) copy-start(f32[5,135,135]{2,1,0:T(8,128)} %param.17) | copy-start | bytes 1093504
  12.4 15.6 %copy-start.4 = (f32[5,135,135]{2,1,0:T(8,128)S(1)}, f32[5,135,135]{2,1,0:T(8,128)}, u32[]{:S(2)}) copy-start(f32[5,135,135]{2,1,0:T(8,128)} %param.18) | copy-start | bytes 1093504
  29.4 0.9 copy-start.10
  30.4 1.0 copy-start.39
  30.4 1.1 copy-start.40
  44.8 2.1 %copy-start.35 = (f32[135,45]{0,1:T(8,128)S(1)}, f32[135,45]{0,1:T(8,128)}, u32[]{:S(2)}) copy-start(f32[135,45]{0,1:T(8,128)} %param.22) | copy-start | bytes 72904
  44.8 2.1 %copy-start.37 = (f32[5,256]{1,0:T(8,128)S(1)}, f32[5,256]{1,0:T(8,128)}, u32[]{:S(2)}) copy-start(f32[5,256]{1,0:T(8,128)} %and_convert_fusion) | copy-start | bytes 15364
  46.9 2.2 %copy-start.7 = (f32[5,135,135]{2,1,0:T(8,128)S(1)}, f32[5,135,135]{2,1,0:T(8,128)}, u32[]{:S(2)}) copy-start(f32[5,135,135]{2,1,0:T(8,128)} %param.17) | copy-start | bytes 1093504
  52.4 12.8 %copy-start.29 = (f32[256,135]{0,1:T(8,128)}, f32[256,135]{0,1:T(8,128)S(1)}, u32[]{:S(2)}) copy-start(f32[256,135]{0,1:T(8,128)S(1)} %fusion.74) | copy-start | bytes 414724
  65.2 1.3 %copy-start.22 = (f32[135,135]{1,0:T(8,128)S(1)}, f32[135,135]{1,0:T(8,128)}, u32[]{:S(2)}) copy-start(f32[135,135]{1,0:T(8,128)} %copy-done.21) | copy-start | bytes 218704
  65.2 1.3 %copy-start.30 = (f32[256,135]{0,1:T(8,128)S(1)}, f32[256,135]{0,1:T(8,128)}, u32[]{:S(2)}) copy-start(f32[256,135]{0,1:T(8,128)} %copy-done.29) | copy-start | bytes 414724
  66.6 0.9 copy-start.20
  66.6 1.0 copy-start.28
  67.5 0.9 copy-start.18
  67.5 1.0 copy-start.26
  67.5 1.5 %copy-start.16 = (f32[135,135]{1,0:T(8,128)S(1)}, f32[135,135]{1,0:T(8,128)}, u32[]{:S(2)}) copy-start(f32[135,135]{1,0:T(8,128)} %copy-done.15) | copy-start | bytes 218704
  67.6 1.5 %copy-start.24 = (f32[256,135]{0,1:T(8,128)S(1)}, f32[256,135]{0,1:T(8,128)}, u32[]{:S(2)}) copy-start(f32[256,135]{0,1:T(8,128)} %copy-done.23) | copy-start | bytes 414724
  68.5 1.7 %copy-start.5 = (f32[5,135,135]{2,1,0:T(8,128)S(1)}, f32[5,135,135]{2,1,0:T(8,128)}, u32[]{:S(2)}) copy-start(f32[5,135,135]{2,1,0:T(8,128)} %param.18) | copy-start | bytes 1093504
  69.0 0.9 copy-start.14
  83.4 1.3 %copy-start.12 = (f32[135,135]{1,0:T(8,128)S(1)}, f32[135,135]{1,0:T(8,128)}, u32[]{:S(2)}) copy-start(f32[135,135]{1,0:T(8,128)} %convolution_negate_fusion) | copy-start | bytes 218704
  84.7 0.9 copy-start.11
  88.8 13.7 %copy-start.2 = (f32[5,135,256]{2,1,0:T(8,128)}, f32[5,135,256]{2,1,0:T(8,128)S(1)}, u32[]{:S(2)}) copy-start(f32[5,135,256]{2,1,0:T(8,128)S(1)} %broadcast_multiply_fusion) | copy-start | bytes 2073604
  90.3 20.7 %copy-start.34 = (f32[135,45]{0,1:T(8,128)S(1)}, f32[135,45]{0,1:T(8,128)}, u32[]{:S(2)}) copy-start(f32[135,45]{0,1:T(8,128)} %param.23) | copy-start | bytes 72904
  90.3 20.7 %collective-permute-start.2 = (f32[2,5,45,1]{3,2,1,0:T(8,128)S(1)}, f32[2,5,45,1]{3,2,1,0:T(8,128)S(1)}, u32[]{:S(2)}, u32[]{:S(2)}) collective-permute-start(f32[2,5,45,1]{3,2,1,0:T(8,128)S(1)} %get-tuple-element.297), channel_id=1, source_target_pairs={{1,0},{2,1},{3,2},{4,3},{5,4},{6,5},{7,6},{0,7},{9,8},{10,9},{11,1... | collective-permute-start | bytes 5408 | tf_op jit(solution)/shard_map/ppermute | solution.py:18
  103.2 8.6 %copy-start.36 = (f32[135,45]{0,1:T(8,128)S(1)}, f32[135,45]{0,1:T(8,128)}, u32[]{:S(2)}) copy-start(f32[135,45]{0,1:T(8,128)} %param.22) | copy-start | bytes 72904
  103.2 8.6 %collective-permute-start.3 = (f32[2,5,45,1]{3,2,1,0:T(8,128)S(1)}, f32[2,5,45,1]{3,2,1,0:T(8,128)S(1)}, u32[]{:S(2)}, u32[]{:S(2)}) collective-permute-start(f32[2,5,45,1]{3,2,1,0:T(8,128)S(1)} %get-tuple-element.296), channel_id=1, source_target_pairs={{0,1},{1,2},{2,3},{3,4},{4,5},{5,6},{6,7},{7,0},{8,9},{9,10},{10,1... | collective-permute-start | bytes 5408 | tf_op jit(solution)/shard_map/ppermute | solution.py:16
  (14 other events, 9.8 us)
where the time goes:
time: 115 us; the launch traced here: 114 us
  blocking collectives  51.5 us (45%)
  matrix products  26.9 us (23%)
  starting transfers between devices  17.2 us (15%)
  local copies, waits for them, and re-layouts  8.73 us (8%)
  waiting for transfers between devices  5.33 us (5%)
  other arithmetic  2.28 us (2%)
  between operations  1.35 us (1%)
    dot_general x44, matrix products, product(): return jnp.dot(left, right, precision=lax.Precision.HIGHEST)  14.8 us
    all_gather x1, blocking collectives, body(): lax.all_gather(spikes[-1][None], 'wall', axis=0, tiled=True)  14.7 us
    all_gather x1, blocking collectives, body(): lax.all_gather(local_rows[-1][None], 'wall', axis=0, tiled=True)  12.8 us
    ppermute x2, starting transfers between devices, padded(): lax.ppermute(head, axis, [((i + 1) % count, i) for i in range(count)])  12.2 us
    dot_general x10, matrix products, batched(): jnp.einsum('fb,kbl->kfl', matrix, field, precision=lax.Precision.HIGHEST)  12.1 us
    all_gather x1, blocking collectives, body(): lax.all_gather(reach_map[0][None], 'wall', axis=0, tiled=True)  12 us
    all_gather x1, blocking collectives, body(): lax.all_gather(back_rows[0][None], 'wall', axis=0, tiled=True)  12 us
    unnamed x86, local copies, waits for them, and re-layouts  8.64 us
  transfers between devices with their start and end apart: 4, of which 1 were waited for; matrix products, arithmetic and copies ran while one was open for 11% of the time, Pallas kernels for 0%

commit v1 on v0

v1 whole, which is shorter than its diff:
```python
import functools

import jax
import jax.numpy as jnp
from jax import lax
from jax.experimental import pallas as pl
from jax.experimental.pallas import tpu as pltpu
from jax.sharding import PartitionSpec as P

section_step = 0.4
MESH = pl.DeviceIdType.MESH
F32 = jnp.float32
BF16 = jnp.bfloat16


def ceil_to(size, unit):
    return (size + unit - 1) // unit * unit


def split(x):
    high = x.astype(BF16)
    return high, (x - high.astype(F32)).astype(BF16)


def dot(a, b):
    return jnp.dot(a, b, preferred_element_type=F32)


def product(matrix, x):
    high, low = matrix
    x_high, x_low = split(x)
    return dot(high, x_high) + (dot(low, x_high) + dot(high, x_low))


def kernel(
    walls,
    streams,
    state,
    pivot_inv,
    lower_block,
    upper_block,
    volume,
    face_minus,
    face_plus,
    lift_minus,
    lift_plus,
    offsets,
    counts,
    out_state,
    out_rate,
    trace_m,
    lift_m,
    step_m,
    upper_m,
    reach_y,
    reach_x,
    exit_m,
    traces,
    rows,
    halo_out,
    halo_in,
    y_out,
    y_in,
    x_out,
    x_in,
    halo_send,
    halo_recv,
    y_send,
    y_recv,
    x_send,
    x_recv,
):
    elements, size, lines = state.shape
    faces = face_minus.shape[0]
    size_pad, face_pad = ceil_to(size, 16), ceil_to(faces, 16)
    chunks = y_out.shape[0]
    width = lines // chunks
    position = lax.axis_index("wall")
    here = lax.axis_index("stream")
    right, left = lax.rem(here + 1, streams), lax.rem(here + streams - 1, streams)

    barrier = pltpu.get_barrier_semaphore()
    pl.semaphore_signal(barrier, inc=1, device_id={"stream": left}, device_id_type=MESH)
    pl.semaphore_signal(barrier, inc=1, device_id={"stream": right}, device_id_type=MESH)

    @pl.when(position > 0)
    def _():
        pl.semaphore_signal(barrier, inc=1, device_id={"wall": position - 1}, device_id_type=MESH)

    @pl.when(position < walls - 1)
    def _():
        pl.semaphore_signal(barrier, inc=1, device_id={"wall": position + 1}, device_id_type=MESH)

    inner = jnp.logical_and(position > 0, position < walls - 1)

    @pl.when(inner)
    def _():
        pl.semaphore_wait(barrier, 4)

    @pl.when(jnp.logical_not(inner))
    def _():
        pl.semaphore_wait(barrier, 3)

    def put(ref, index, value):
        high, low = split(value)
        ref[0, index] = high
        ref[1, index] = low

    def take(ref, index):
        return ref[0, index], ref[1, index]

    trace_m[...] = jnp.zeros_like(trace_m)
    lift_m[...] = jnp.zeros_like(lift_m)
    for first, ref in ((0, volume), (size_pad, face_minus), (size_pad + face_pad, face_plus)):
        high, low = split(ref[...])
        trace_m[0, first : first + ref.shape[0], :] = high
        trace_m[1, first : first + ref.shape[0], :] = low
    for which, ref in ((0, lift_plus), (1, lift_minus)):
        high, low = split(ref[...])
        lift_m[0, which, :, :faces] = high
        lift_m[1, which, :, :faces] = low

    lane = lax.broadcasted_iota(jnp.int32, (face_pad, lines), 1)
    narrow = lax.broadcasted_iota(jnp.int32, (face_pad, halo_out.shape[2]), 1)

    def halo_copy(turn, side):
        slot = 2 * turn + side
        return pltpu.make_async_remote_copy(
            src_ref=halo_out.at[slot],
            dst_ref=halo_in.at[slot],
            send_sem=halo_send.at[slot],
            recv_sem=halo_recv.at[slot],
            device_id={"stream": left if side == 0 else right},
            device_id_type=MESH,
        )

    def start_rate(field, turn):
        first = jnp.zeros((face_pad, halo_out.shape[2]), F32)
        last = jnp.zeros((face_pad, halo_out.shape[2]), F32)
        for k in range(elements):
            out = product((trace_m[0], trace_m[1]), field(k))
            traces[k] = out
            low = out[size_pad : size_pad + face_pad]
            high = out[size_pad + face_pad :]
            first = jnp.where(narrow == k, low[:, :1], first)
            last = jnp.where(narrow == k, high[:, lines - 1 :], last)
        halo_out[2 * turn] = first
        halo_out[2 * turn + 1] = last
        halo_copy(turn, 0).start()
        halo_copy(turn, 1).start()

    def wait_rate(turn):
        halo_copy(turn, 0).wait()
        halo_copy(turn, 1).wait()

    def rate(k, turn):
        low = traces[k, size_pad : size_pad + face_pad, :]
        high = traces[k, size_pad + face_pad :, :]
        low_next = halo_in[2 * turn][:, k : k + 1]
        high_prev = halo_in[2 * turn + 1][:, k : k + 1]
        up = jnp.where(lane == lines - 1, low_next, pltpu.roll(low, lines - 1, 1)) - high
        down = low - jnp.where(lane == 0, high_prev, pltpu.roll(high, 1, 1))
        return (
            traces[k, :size, :]
            + product((lift_m[0, 0], lift_m[1, 0]), up)
            + product((lift_m[0, 1], lift_m[1, 1]), down)
        )

    begin = offsets[...]
    end = begin + counts[...]

    def active(k):
        element = position * elements + k
        return ((begin <= element) & (element < end)).astype(F32)

    start_rate(lambda k: state[k], 0)

    for k in range(elements):
        step = product(split(pivot_inv[k]), lower_block[k])
        put(step_m, k, step)
        put(upper_m, k, upper_block[k])
    spikes = [-(step_m[0, 0].astype(F32) + step_m[1, 0].astype(F32))]
    for k in range(1, elements):
        spikes.append(-product(take(step_m, k), spikes[-1]))
    put(exit_m, 0, spikes[-1])
    map_y, map_x = spikes[-1], -upper_block[elements - 1]
    put(reach_y, elements - 1, map_y)
    put(reach_x, elements - 1, map_x)
    for k in reversed(range(elements - 1)):
        map_y = spikes[k] - product(take(upper_m, k), map_y)
        map_x = -product(take(upper_m, k), map_x)
        put(reach_y, k, map_y)
        put(reach_x, k, map_x)

    wait_rate(0)
    local = None
    for k in range(elements):
        right_side = active(k) * (state[k] + section_step * rate(k, 0))
        forced = product(split(pivot_inv[k]), right_side)
        local = forced if k == 0 else forced - product(take(step_m, k), local)
        rows[k] = local

    def y_copy(c):
        return pltpu.make_async_remote_copy(
            src_ref=y_out.at[c],
            dst_ref=y_in.at[c],
            send_sem=y_send.at[c],
            recv_sem=y_recv.at[c],
            device_id={"wall": lax.rem(position + 1, walls)},
            device_id_type=MESH,
        )

    def x_copy(c):
        return pltpu.make_async_remote_copy(
            src_ref=x_out.at[c],
            dst_ref=x_in.at[c],
            send_sem=x_send.at[c],
            recv_sem=x_recv.at[c],
            device_id={"wall": lax.rem(position + walls - 1, walls)},
            device_id_type=MESH,
        )

    columns = [slice(c * width, (c + 1) * width) for c in range(chunks)]

    @pl.when(position == 0)
    def _():
        for c in range(chunks):
            y_out[c] = rows[elements - 1, :, columns[c]]
            y_copy(c).start()
            y_in[c] = jnp.zeros_like(y_in[c])

    @pl.when(position == walls - 1)
    def _():
        for c in range(chunks):
            x_in[c] = jnp.zeros_like(x_in[c])

    last_rows = [rows[elements - 1, :, columns[c]] for c in range(chunks)]
    after = rows[elements - 1]
    for k in reversed(range(elements - 1)):
        after = rows[k] - product(take(upper_m, k), after)
        rows[k] = after

    for c in range(chunks):

        @pl.when(position > 0)
        def _():
            y_copy(c).wait_recv()

            @pl.when(position < walls - 1)
            def _():
                y_out[c] = last_rows[c] + product(take(exit_m, 0), y_in[c])
                y_copy(c).start()

        @pl.when(position == walls - 1)
        def _():
            x_out[c] = rows[0, :, columns[c]] + product(take(reach_y, 0), y_in[c])
            x_copy(c).start()

    for c in range(chunks):
        for k in range(elements):
            rows[k, :, columns[c]] = rows[k, :, columns[c]] + product(take(reach_y, k), y_in[c])

    for c in range(chunks):

        @pl.when(position < walls - 1)
        def _():
            x_copy(c).wait_recv()

            @pl.when(position > 0)
            def _():
                x_out[c] = rows[0, :, columns[c]] + product(take(reach_x, 0), x_in[c])
                x_copy(c).start()

    for k in range(elements):
        for c in range(chunks):
            solved = rows[k, :, columns[c]] + product(take(reach_x, k), x_in[c])
            out_state[k, :, columns[c]] = active(k)[:, columns[c]] * solved

    start_rate(lambda k: out_state[k], 1)

    @pl.when(position < walls - 1)
    def _():
        for c in range(chunks):
            y_copy(c).wait_send()

    @pl.when(position > 0)
    def _():
        for c in range(chunks):
            x_copy(c).wait_send()

    wait_rate(1)
    for k in range(elements):
        out_rate[k] = active(k) * rate(k, 1)


def solution(mesh):
    walls, streams = mesh.shape["wall"], mesh.shape["stream"]

    def body(
        state,
        pivot_inv,
        lower_block,
        upper_block,
        volume,
        face_minus,
        face_plus,
        lift_minus,
        lift_plus,
        offsets,
        counts,
    ):
        elements, size, lines = state.shape
        faces = face_minus.shape[0]
        size_pad, face_pad = ceil_to(size, 16), ceil_to(faces, 16)
        chunks = 2 if lines % 256 == 0 else 1
        width = lines // chunks
        halo_width = ceil_to(elements, 128)
        vmem = pl.BlockSpec(memory_space=pltpu.VMEM)
        return pl.pallas_call(
            functools.partial(kernel, walls, streams),
            out_shape=(jax.ShapeDtypeStruct(state.shape, F32),) * 2,
            in_specs=[vmem] * 11,
            out_specs=(vmem, vmem),
            scratch_shapes=[
                pltpu.VMEM((2, size_pad + 2 * face_pad, size), BF16),
                pltpu.VMEM((2, 2, size, face_pad), BF16),
                pltpu.VMEM((2, elements, size, size), BF16),
                pltpu.VMEM((2, elements, size, size), BF16),
                pltpu.VMEM((2, elements, size, size), BF16),
                pltpu.VMEM((2, elements, size, size), BF16),
                pltpu.VMEM((2, 1, size, size), BF16),
                pltpu.VMEM((elements, size_pad + 2 * face_pad, lines), F32),
                pltpu.VMEM((elements, size, lines), F32),
                pltpu.VMEM((4, face_pad, halo_width), F32),
                pltpu.VMEM((4, face_pad, halo_width), F32),
                pltpu.VMEM((chunks, size, width), F32),
                pltpu.VMEM((chunks, size, width), F32),
                pltpu.VMEM((chunks, size, width), F32),
                pltpu.VMEM((chunks, size, width), F32),
                pltpu.SemaphoreType.DMA((4,)),
                pltpu.SemaphoreType.DMA((4,)),
                pltpu.SemaphoreType.DMA((chunks,)),
                pltpu.SemaphoreType.DMA((chunks,)),
                pltpu.SemaphoreType.DMA((chunks,)),
                pltpu.SemaphoreType.DMA((chunks,)),
            ],
            compiler_params=pltpu.CompilerParams(
                collective_id=0, has_side_effects=True, vmem_limit_bytes=32 * 1024 * 1024
            ),
        )(
            state,
            pivot_inv,
            lower_block,
            upper_block,
            volume,
            face_minus,
            face_plus,
            lift_minus,
            lift_plus,
            offsets.reshape(1, lines),
            counts.reshape(1, lines),
        )

    in_specs = (
        P("wall", None, "stream"),
        P("wall", None, None),
        P("wall", None, None),
        P("wall", None, None),
        P(),
        P(),
        P(),
        P(),
        P(),
        P("stream"),
        P("stream"),
    )
    out_specs = (P("wall", None, "stream"), P("wall", None, "stream"))
    return jax.shard_map(body, mesh=mesh, in_specs=in_specs, out_specs=out_specs, check_vma=False)
```

time: 115 us -> 46.5 us (0.40)
  blocking collectives: 51.5 us -> 0 us
  Pallas kernels: 0 us -> 37.4 us
  matrix products: 26.9 us -> 0 us
  starting transfers between devices: 17.2 us -> 0 us
  waiting for transfers between devices: 5.33 us -> 0 us
  other arithmetic: 2.28 us -> 0 us
    all_gather x4 -> x0, blocking collectives: 51.5 us -> none  [the longest x1 14.7 us: body(): lax.all_gather(spikes[-1][None], 'wall', axis=0, tiled=True)]
    pallas_call x0 -> x1, Pallas kernels: none -> 37.4 us  [body(): pl.pallas_call(functools.partial(kernel, walls, streams), out_shape=(jax....]
    dot_general x54 -> x0, matrix products: 26.9 us -> none  [the longest x44 14.8 us: product(): return jnp.dot(left, right, precision=lax.Precision.HIGHEST)]
    ppermute x4 -> x0, starting transfers between devices: 17.2 us -> none  [the longest x2 12.2 us: padded(): lax.ppermute(head, axis, [((i + 1) % count, i) for i in range(count)])]
    ppermute x4 -> x0, waiting for transfers between devices: 5.33 us -> none  [the longest x2 5.33 us: padded(): lax.ppermute(head, axis, [((i + 1) % count, i) for i in range(count)])]
    unnamed x86 -> x22, local copies, waits for them, and re-layouts: 8.64 us -> 8 us
  transfers between devices with their start and end apart: 4 -> 0, of which waited for: 1 -> 0; matrix products, arithmetic and copies ran while one was open for 11% -> 0% of each run, Pallas kernels for 0% -> 0%
where the time goes in v1:
time: 46.5 us; the launch traced here: 46.2 us
  Pallas kernels  37.4 us (80%)
  local copies, waits for them, and re-layouts  8 us (17%)
  between operations  0.72 us (2%)
    pallas_call x1, Pallas kernels, body(): pl.pallas_call(functools.partial(kernel, walls, streams), out_shape=(jax....  37.4 us
    unnamed x22, local copies, waits for them, and re-layouts  8 us

profile of v1, /device:TPU:1, one launch (start us, length us, event | category | flops | bytes accessed | tf_op | source)
XLA Modules:
  0.0 46.2 jit_solution(13923989817117070044)
XLA Ops:
  0.6 0.0 copy-start.4
  0.6 0.9 %copy.13.lift_minus = f32[135,45]{1,0:T(8,128)S(1)} copy(f32[135,45]{0,1:T(8,128)} %param.18) | data formatting | bytes 48600 | tf_op args[7]
  1.6 0.0 copy-start.5
  1.6 0.0 copy-start.6
  1.6 0.0 copy-start.7
  1.6 0.0 copy-start.8
  1.6 0.9 %copy.14.lift_plus = f32[135,45]{1,0:T(8,128)S(1)} copy(f32[135,45]{0,1:T(8,128)} %param.19) | data formatting | bytes 48600 | tf_op args[8]
  2.6 0.0 copy-done.4
  2.6 0.0 copy-done.5
  2.6 0.0 copy-done.6
  2.6 0.0 copy-done.7
  2.6 0.0 copy-done.8
  2.6 0.0 copy-start
  2.6 1.1 %copy-done = f32[5,135,256]{2,1,0:T(8,128)S(1)} copy-done((f32[5,135,256]{2,1,0:T(8,128)S(1)}, f32[5,135,256]{2,1,0:T(8,128)}, u32[]{:S(2)}) %copy-start) | copy-done | bytes 691224
  3.7 0.0 copy-start.1
  3.7 1.1 %copy-done.1 = f32[5,135,135]{2,1,0:T(8,128)S(1)} copy-done((f32[5,135,135]{2,1,0:T(8,128)S(1)}, f32[5,135,135]{2,1,0:T(8,128)}, u32[]{:S(2)}) %copy-start.1) | copy-done | bytes 364524
  4.8 0.0 copy-start.2
  4.8 1.1 %copy-done.2 = f32[5,135,135]{2,1,0:T(8,128)S(1)} copy-done((f32[5,135,135]{2,1,0:T(8,128)S(1)}, f32[5,135,135]{2,1,0:T(8,128)}, u32[]{:S(2)}) %copy-start.2) | copy-done | bytes 364524
  5.9 0.0 copy-start.3
  5.9 1.1 %copy-done.3 = f32[5,135,135]{2,1,0:T(8,128)S(1)} copy-done((f32[5,135,135]{2,1,0:T(8,128)S(1)}, f32[5,135,135]{2,1,0:T(8,128)}, u32[]{:S(2)}) %copy-start.3) | copy-done | bytes 364524
  7.0 37.4 %shard_map.122 = (f32[5,135,256]{2,1,0:T(8,128)S(1)}, f32[5,135,256]{2,1,0:T(8,128)S(1)}) custom-call(f32[5,135,256]{2,1,0:T(8,128)S(1)} %copy-done, f32[5,135,135]{2,1,0:T(8,128)S(1)} %copy-done.1, f32[5,135,135]{2,1,0:T(8,128)S(1)} %copy-done.2, f32[5,135,135]{2,1,0:T(8,128)S(1)} %copy-done.3, f32[135,135]{1,0:T(8,128)S(1)} %copy-done.4, ...), custom_call_target="tpu_custom_call" | custom-call | tf_op jit(solution)/shard_map/pallas_call | solution.py:319
  44.5 0.9 %copy.17 = f32[5,135,256]{2,1,0:T(8,128)} copy(f32[5,135,256]{2,1,0:T(8,128)S(1)} %get-tuple-element.4) | data formatting | bytes 1382400
  45.3 0.8 %copy.18 = f32[5,135,256]{2,1,0:T(8,128)} copy(f32[5,135,256]{2,1,0:T(8,128)S(1)} %get-tuple-element.5) | data formatting | bytes 1382400
Async XLA Ops:
  0.6 1.9 %copy-start.4 = (f32[135,135]{1,0:T(8,128)S(1)}, f32[135,135]{1,0:T(8,128)}, u32[]{:S(2)}) copy-start(f32[135,135]{1,0:T(8,128)} %volume.1) | copy-start | bytes 218704
  1.6 1.0 %copy-start.5 = (f32[45,135]{1,0:T(8,128)S(1)}, f32[45,135]{1,0:T(8,128)}, u32[]{:S(2)}) copy-start(f32[45,135]{1,0:T(8,128)} %face_minus.1) | copy-start | bytes 72904
  1.6 1.0 %copy-start.6 = (f32[45,135]{1,0:T(8,128)S(1)}, f32[45,135]{1,0:T(8,128)}, u32[]{:S(2)}) copy-start(f32[45,135]{1,0:T(8,128)} %face_plus.1) | copy-start | bytes 72904
  1.6 1.0 %copy-start.7 = (s32[256]{0:T(256)S(1)}, s32[256]{0:T(256)}, u32[]{:S(2)}) copy-start(s32[256]{0:T(256)} %param.20) | copy-start | bytes 3076
  1.6 1.0 %copy-start.8 = (s32[256]{0:T(256)S(1)}, s32[256]{0:T(256)}, u32[]{:S(2)}) copy-start(s32[256]{0:T(256)} %param.21) | copy-start | bytes 3076
  2.6 1.1 %copy-start = (f32[5,135,256]{2,1,0:T(8,128)S(1)}, f32[5,135,256]{2,1,0:T(8,128)}, u32[]{:S(2)}) copy-start(f32[5,135,256]{2,1,0:T(8,128)} %state.1) | copy-start | bytes 2073604
  3.7 1.1 %copy-start.1 = (f32[5,135,135]{2,1,0:T(8,128)S(1)}, f32[5,135,135]{2,1,0:T(8,128)}, u32[]{:S(2)}) copy-start(f32[5,135,135]{2,1,0:T(8,128)} %pivot_inv.1) | copy-start | bytes 1093504
  4.8 1.1 %copy-start.2 = (f32[5,135,135]{2,1,0:T(8,128)S(1)}, f32[5,135,135]{2,1,0:T(8,128)}, u32[]{:S(2)}) copy-start(f32[5,135,135]{2,1,0:T(8,128)} %lower_block.1) | copy-start | bytes 1093504
  5.9 1.1 %copy-start.3 = (f32[5,135,135]{2,1,0:T(8,128)S(1)}, f32[5,135,135]{2,1,0:T(8,128)}, u32[]{:S(2)}) copy-start(f32[5,135,135]{2,1,0:T(8,128)} %upper_block.1) | copy-start | bytes 1093504

commit v2 on v1

--- a/solution.py
+++ b/solution.py
@@ -35,6 +35,19 @@
 def kernel(
     walls,
     streams,
+    state_hbm,
+    pivot_hbm,
+    lower_hbm,
+    upper_hbm,
+    volume_hbm,
+    minus_hbm,
+    plus_hbm,
+    lift_minus_hbm,
+    lift_plus_hbm,
+    offsets_hbm,
+    counts_hbm,
+    out_state,
+    out_rate,
     state,
     pivot_inv,
     lower_block,
@@ -46,8 +59,7 @@
     lift_plus,
     offsets,
     counts,
-    out_state,
-    out_rate,
+    load_sem,
     trace_m,
     lift_m,
     step_m,
@@ -63,12 +75,18 @@
     y_in,
     x_out,
     x_in,
+    last,
+    m_out,
+    m_in,
+    down_m,
     halo_send,
     halo_recv,
     y_send,
     y_recv,
     x_send,
     x_recv,
+    m_send,
+    m_recv,
 ):
     elements, size, lines = state.shape
     faces = face_minus.shape[0]
@@ -79,6 +97,27 @@
     here = lax.axis_index("stream")
     right, left = lax.rem(here + 1, streams), lax.rem(here + streams - 1, streams)
 
+    half = walls // 2
+    sources = (
+        (volume_hbm, volume),
+        (minus_hbm, face_minus),
+        (plus_hbm, face_plus),
+        (state_hbm, state),
+        (pivot_hbm, pivot_inv),
+        (lower_hbm, lower_block),
+        (upper_hbm, upper_block),
+        (lift_minus_hbm, lift_minus),
+        (lift_plus_hbm, lift_plus),
+        (offsets_hbm, offsets),
+        (counts_hbm, counts),
+    )
+    loads = [
+        pltpu.make_async_copy(source, target, load_sem.at[i])
+        for i, (source, target) in enumerate(sources)
+    ]
+    for load in loads:
+        load.start()
+
     barrier = pltpu.get_barrier_semaphore()
     pl.semaphore_signal(barrier, inc=1, device_id={"stream": left}, device_id_type=MESH)
     pl.semaphore_signal(barrier, inc=1, device_id={"stream": right}, device_id_type=MESH)
@@ -111,15 +150,12 @@
 
     trace_m[...] = jnp.zeros_like(trace_m)
     lift_m[...] = jnp.zeros_like(lift_m)
+    for load in loads[:3]:
+        load.wait()
     for first, ref in ((0, volume), (size_pad, face_minus), (size_pad + face_pad, face_plus)):
         high, low = split(ref[...])
         trace_m[0, first : first + ref.shape[0], :] = high
         trace_m[1, first : first + ref.shape[0], :] = low
-    for which, ref in ((0, lift_plus), (1, lift_minus)):
-        high, low = split(ref[...])
-        lift_m[0, which, :, :faces] = high
-        lift_m[1, which, :, :faces] = low
-
     lane = lax.broadcasted_iota(jnp.int32, (face_pad, lines), 1)
     narrow = lax.broadcasted_iota(jnp.int32, (face_pad, halo_out.shape[2]), 1)
 
@@ -136,16 +172,16 @@
 
     def start_rate(field, turn):
         first = jnp.zeros((face_pad, halo_out.shape[2]), F32)
-        last = jnp.zeros((face_pad, halo_out.shape[2]), F32)
+        final = jnp.zeros((face_pad, halo_out.shape[2]), F32)
         for k in range(elements):
             out = product((trace_m[0], trace_m[1]), field(k))
             traces[k] = out
             low = out[size_pad : size_pad + face_pad]
             high = out[size_pad + face_pad :]
             first = jnp.where(narrow == k, low[:, :1], first)
-            last = jnp.where(narrow == k, high[:, lines - 1 :], last)
+            final = jnp.where(narrow == k, high[:, lines - 1 :], final)
         halo_out[2 * turn] = first
-        halo_out[2 * turn + 1] = last
+        halo_out[2 * turn + 1] = final
         halo_copy(turn, 0).start()
         halo_copy(turn, 1).start()
 
@@ -166,14 +202,21 @@
             + product((lift_m[0, 1], lift_m[1, 1]), down)
         )
 
-    begin = offsets[...]
-    end = begin + counts[...]
 
     def active(k):
         element = position * elements + k
         return ((begin <= element) & (element < end)).astype(F32)
 
+    loads[3].wait()
     start_rate(lambda k: state[k], 0)
+    for load in loads[4:]:
+        load.wait()
+    begin = offsets[...]
+    end = begin + counts[...]
+    for which, ref in ((0, lift_plus), (1, lift_minus)):
+        high, low = split(ref[...].T)
+        lift_m[0, which, :, :faces] = high
+        lift_m[1, which, :, :faces] = low
 
     for k in range(elements):
         step = product(split(pivot_inv[k]), lower_block[k])
@@ -192,6 +235,21 @@
         put(reach_y, k, map_y)
         put(reach_x, k, map_x)
 
+    def m_copy():
+        return pltpu.make_async_remote_copy(
+            src_ref=m_out,
+            dst_ref=m_in,
+            send_sem=m_send,
+            recv_sem=m_recv,
+            device_id={"wall": lax.rem(position + walls - 1, walls)},
+            device_id_type=MESH,
+        )
+
+    @pl.when(position == walls - 1)
+    def _():
+        m_out[...] = map_y
+        m_copy().start()
+
     wait_rate(0)
     local = None
     for k in range(elements):
@@ -227,43 +285,78 @@
         for c in range(chunks):
             y_out[c] = rows[elements - 1, :, columns[c]]
             y_copy(c).start()
-            y_in[c] = jnp.zeros_like(y_in[c])
-
-    @pl.when(position == walls - 1)
-    def _():
-        for c in range(chunks):
-            x_in[c] = jnp.zeros_like(x_in[c])
-
-    last_rows = [rows[elements - 1, :, columns[c]] for c in range(chunks)]
+
+    last[...] = rows[elements - 1]
     after = rows[elements - 1]
     for k in reversed(range(elements - 1)):
         after = rows[k] - product(take(upper_m, k), after)
         rows[k] = after
 
-    for c in range(chunks):
-
-        @pl.when(position > 0)
-        def _():
+    @pl.when(position == walls - 1)
+    def _():
+        for c in range(chunks):
+            x_out[c] = rows[0, :, columns[c]]
+            x_copy(c).start()
+
+    @pl.when(jnp.logical_and(position >= half, position < walls - 1))
+    def _():
+        m_copy().wait_recv()
+        through = product(take(reach_x, 0), m_in[...])
+        put(down_m, 0, through)
+        m_out[...] = (reach_y[0, 0].astype(F32) + reach_y[1, 0].astype(F32)) + product(
+            take(down_m, 0), spikes[-1]
+        )
+        m_copy().start()
+        above = rows[0] + product(take(down_m, 0), last[...])
+        for c in range(chunks):
+            x_copy(c).wait_recv()
+            x_out[c] = above[:, columns[c]] + product(take(reach_x, 0), x_in[c])
+            x_copy(c).start()
+
+    @pl.when(jnp.logical_and(position > 0, position < half))
+    def _():
+        for c in range(chunks):
+            y_copy(c).wait_recv()
+            y_out[c] = last[:, columns[c]] + product(take(exit_m, 0), y_in[c])
+            y_copy(c).start()
+
+    @pl.when(position >= half)
+    def _():
+        for c in range(chunks):
             y_copy(c).wait_recv()
 
             @pl.when(position < walls - 1)
             def _():
-                y_out[c] = last_rows[c] + product(take(exit_m, 0), y_in[c])
+                y_out[c] = last[:, columns[c]] + product(take(exit_m, 0), y_in[c])
                 y_copy(c).start()
-
-        @pl.when(position == walls - 1)
-        def _():
-            x_out[c] = rows[0, :, columns[c]] + product(take(reach_y, 0), y_in[c])
-            x_copy(c).start()
-
-    for c in range(chunks):
-        for k in range(elements):
-            rows[k, :, columns[c]] = rows[k, :, columns[c]] + product(take(reach_y, k), y_in[c])
-
-    for c in range(chunks):
-
-        @pl.when(position < walls - 1)
-        def _():
+                x_in[c] = x_in[c] + product(split(m_in[...]), y_out[c])
+
+    @pl.when(position == half - 1)
+    def _():
+        m_copy().wait_recv()
+        for c in range(chunks):
+            met = product(split(m_in[...]), y_out[c])
+            x_copy(c).wait_recv()
+            x_in[c] = x_in[c] + met
+
+            @pl.when(position > 0)
+            def _():
+                x_out[c] = (
+                    rows[0, :, columns[c]]
+                    + product(take(reach_y, 0), y_in[c])
+                    + product(take(reach_x, 0), x_in[c])
+                )
+                x_copy(c).start()
+
+    @pl.when(position > 0)
+    def _():
+        for c in range(chunks):
+            for k in range(elements):
+                rows[k, :, columns[c]] += product(take(reach_y, k), y_in[c])
+
+    @pl.when(position < half - 1)
+    def _():
+        for c in range(chunks):
             x_copy(c).wait_recv()
 
             @pl.when(position > 0)
@@ -271,10 +364,14 @@
                 x_out[c] = rows[0, :, columns[c]] + product(take(reach_x, 0), x_in[c])
                 x_copy(c).start()
 
+    @pl.when(position < walls - 1)
+    def _():
+        for c in range(chunks):
+            for k in range(elements):
+                rows[k, :, columns[c]] += product(take(reach_x, k), x_in[c])
+
     for k in range(elements):
-        for c in range(chunks):
-            solved = rows[k, :, columns[c]] + product(take(reach_x, k), x_in[c])
-            out_state[k, :, columns[c]] = active(k)[:, columns[c]] * solved
+        out_state[k] = active(k) * rows[k]
 
     start_rate(lambda k: out_state[k], 1)
 
@@ -287,6 +384,10 @@
     def _():
         for c in range(chunks):
             x_copy(c).wait_send()
+
+    @pl.when(position >= half)
+    def _():
+        m_copy().wait_send()
 
     wait_rate(1)
     for k in range(elements):
@@ -316,12 +417,27 @@
         width = lines // chunks
         halo_width = ceil_to(elements, 128)
         vmem = pl.BlockSpec(memory_space=pltpu.VMEM)
+        operands = (
+            state,
+            pivot_inv,
+            lower_block,
+            upper_block,
+            volume,
+            face_minus,
+            face_plus,
+            lift_minus.T,
+            lift_plus.T,
+            offsets.reshape(1, lines),
+            counts.reshape(1, lines),
+        )
         return pl.pallas_call(
             functools.partial(kernel, walls, streams),
             out_shape=(jax.ShapeDtypeStruct(state.shape, F32),) * 2,
-            in_specs=[vmem] * 11,
+            in_specs=[pl.BlockSpec(memory_space=pltpu.HBM)] * 11,
             out_specs=(vmem, vmem),
-            scratch_shapes=[
+            scratch_shapes=[pltpu.VMEM(x.shape, x.dtype) for x in operands]
+            + [
+                pltpu.SemaphoreType.DMA((len(operands),)),
                 pltpu.VMEM((2, size_pad + 2 * face_pad, size), BF16),
                 pltpu.VMEM((2, 2, size, face_pad), BF16),
                 pltpu.VMEM((2, elements, size, size), BF16),
@@ -337,29 +453,23 @@
                 pltpu.VMEM((chunks, size, width), F32),
                 pltpu.VMEM((chunks, size, width), F32),
                 pltpu.VMEM((chunks, size, width), F32),
+                pltpu.VMEM((size, lines), F32),
+                pltpu.VMEM((size, size), F32),
+                pltpu.VMEM((size, size), F32),
+                pltpu.VMEM((2, 1, size, size), BF16),
                 pltpu.SemaphoreType.DMA((4,)),
                 pltpu.SemaphoreType.DMA((4,)),
                 pltpu.SemaphoreType.DMA((chunks,)),
                 pltpu.SemaphoreType.DMA((chunks,)),
                 pltpu.SemaphoreType.DMA((chunks,)),
                 pltpu.SemaphoreType.DMA((chunks,)),
+                pltpu.SemaphoreType.DMA,
+                pltpu.SemaphoreType.DMA,
             ],
             compiler_params=pltpu.CompilerParams(
                 collective_id=0, has_side_effects=True, vmem_limit_bytes=32 * 1024 * 1024
             ),
-        )(
-            state,
-            pivot_inv,
-            lower_block,
-            upper_block,
-            volume,
-            face_minus,
-            face_plus,
-            lift_minus,
-            lift_plus,
-            offsets.reshape(1, lines),
-            counts.reshape(1, lines),
-        )
+        )(*operands)
 
     in_specs = (
         P("wall", None, "stream"),

time: 46.5 us -> 43.2 us (0.929)
  Pallas kernels: 37.4 us -> 31.1 us
  local copies, waits for them, and re-layouts: 8 us -> 10.9 us
    pallas_call x1, Pallas kernels: 37.4 us -> 31.1 us  [body(): pl.pallas_call(functools.partial(kernel, walls, streams), out_shape=(jax....]
    unnamed x22 -> x24, local copies, waits for them, and re-layouts: 8 us -> 10.9 us
where the time goes in v2:
time: 43.2 us; the launch traced here: 42.7 us
  Pallas kernels  31.1 us (72%)
  local copies, waits for them, and re-layouts  10.9 us (25%)
  between operations  0.67 us (2%)
    pallas_call x1, Pallas kernels, body(): pl.pallas_call(functools.partial(kernel, walls, streams), out_shape=(jax....  31.1 us
    unnamed x24, local copies, waits for them, and re-layouts  10.9 us

profile of v2, /device:TPU:1, one launch (start us, length us, event | category | flops | bytes accessed | tf_op | source)
XLA Modules:
  0.0 42.7 jit_solution(15324410264424257960)
XLA Ops:
  0.6 0.0 copy-start.10
  0.6 0.0 copy-start.9
  0.7 0.7 %copy-done.10 = s32[256]{0:T(256)S(1)} copy-done((s32[256]{0:T(256)S(1)}, s32[256]{0:T(256)}, u32[]{:S(2)}) %copy-start.10) | copy-done | bytes 1048
  1.3 0.0 copy-done.9
  1.3 0.0 copy-start
  1.3 1.1 %copy-done = f32[5,135,256]{2,1,0:T(8,128)S(1)} copy-done((f32[5,135,256]{2,1,0:T(8,128)S(1)}, f32[5,135,256]{2,1,0:T(8,128)}, u32[]{:S(2)}) %copy-start) | copy-done | bytes 691224
  2.4 0.0 copy-start.1
  2.4 1.1 %copy-done.1 = f32[5,135,135]{2,1,0:T(8,128)S(1)} copy-done((f32[5,135,135]{2,1,0:T(8,128)S(1)}, f32[5,135,135]{2,1,0:T(8,128)}, u32[]{:S(2)}) %copy-start.1) | copy-done | bytes 364524
  3.5 0.0 copy-start.2
  3.5 1.1 %copy-done.2 = f32[5,135,135]{2,1,0:T(8,128)S(1)} copy-done((f32[5,135,135]{2,1,0:T(8,128)S(1)}, f32[5,135,135]{2,1,0:T(8,128)}, u32[]{:S(2)}) %copy-start.2) | copy-done | bytes 364524
  4.6 0.0 copy-start.3
  4.6 1.1 %copy-done.3 = f32[5,135,135]{2,1,0:T(8,128)S(1)} copy-done((f32[5,135,135]{2,1,0:T(8,128)S(1)}, f32[5,135,135]{2,1,0:T(8,128)}, u32[]{:S(2)}) %copy-start.3) | copy-done | bytes 364524
  5.7 0.0 copy-start.4
  5.7 0.9 %copy-done.4 = f32[135,135]{1,0:T(8,128)S(1)} copy-done((f32[135,135]{1,0:T(8,128)S(1)}, f32[135,135]{1,0:T(8,128)}, u32[]{:S(2)}) %copy-start.4) | copy-done | bytes 72924
  6.6 0.0 copy-start.5
  6.6 0.8 %copy-done.5 = f32[45,135]{1,0:T(8,128)S(1)} copy-done((f32[45,135]{1,0:T(8,128)S(1)}, f32[45,135]{1,0:T(8,128)}, u32[]{:S(2)}) %copy-start.5) | copy-done | bytes 24324
  7.4 0.0 copy-start.6
  7.4 0.8 %copy-done.6 = f32[45,135]{1,0:T(8,128)S(1)} copy-done((f32[45,135]{1,0:T(8,128)S(1)}, f32[45,135]{1,0:T(8,128)}, u32[]{:S(2)}) %copy-start.6) | copy-done | bytes 24324
  8.2 0.0 copy-start.7
  8.2 0.8 %copy-done.7 = f32[135,45]{0,1:T(8,128)S(1)} copy-done((f32[135,45]{0,1:T(8,128)S(1)}, f32[135,45]{0,1:T(8,128)}, u32[]{:S(2)}) %copy-start.7) | copy-done | bytes 24324
  9.0 0.0 copy-start.8
  9.0 0.8 %copy-done.8 = f32[135,45]{0,1:T(8,128)S(1)} copy-done((f32[135,45]{0,1:T(8,128)S(1)}, f32[135,45]{0,1:T(8,128)}, u32[]{:S(2)}) %copy-start.8) | copy-done | bytes 24324
  9.8 31.1 %shard_map.122 = (f32[5,135,256]{2,1,0:T(8,128)S(1)}, f32[5,135,256]{2,1,0:T(8,128)S(1)}) custom-call(f32[5,135,256]{2,1,0:T(8,128)S(1)} %copy-done, f32[5,135,135]{2,1,0:T(8,128)S(1)} %copy-done.1, f32[5,135,135]{2,1,0:T(8,128)S(1)} %copy-done.2, f32[5,135,135]{2,1,0:T(8,128)S(1)} %copy-done.3, f32[135,135]{1,0:T(8,128)S(1)} %copy-done.4, ...), custom_call_target="tpu_custom_call" | custom-call | tf_op jit(solution)/shard_map/pallas_call | solution.py:433
  41.0 0.9 %copy.15 = f32[5,135,256]{2,1,0:T(8,128)} copy(f32[5,135,256]{2,1,0:T(8,128)S(1)} %get-tuple-element.4) | data formatting | bytes 1382400
  41.8 0.8 %copy.16 = f32[5,135,256]{2,1,0:T(8,128)} copy(f32[5,135,256]{2,1,0:T(8,128)S(1)} %get-tuple-element.5) | data formatting | bytes 1382400
Async XLA Ops:
  0.6 0.7 %copy-start.10 = (s32[256]{0:T(256)S(1)}, s32[256]{0:T(256)}, u32[]{:S(2)}) copy-start(s32[256]{0:T(256)} %param.21) | copy-start | bytes 3076
  0.6 0.7 %copy-start.9 = (s32[256]{0:T(256)S(1)}, s32[256]{0:T(256)}, u32[]{:S(2)}) copy-start(s32[256]{0:T(256)} %param.20) | copy-start | bytes 3076
  1.3 1.1 %copy-start = (f32[5,135,256]{2,1,0:T(8,128)S(1)}, f32[5,135,256]{2,1,0:T(8,128)}, u32[]{:S(2)}) copy-start(f32[5,135,256]{2,1,0:T(8,128)} %state_hbm.1) | copy-start | bytes 2073604
  2.4 1.1 %copy-start.1 = (f32[5,135,135]{2,1,0:T(8,128)S(1)}, f32[5,135,135]{2,1,0:T(8,128)}, u32[]{:S(2)}) copy-start(f32[5,135,135]{2,1,0:T(8,128)} %pivot_hbm.1) | copy-start | bytes 1093504
  3.5 1.1 %copy-start.2 = (f32[5,135,135]{2,1,0:T(8,128)S(1)}, f32[5,135,135]{2,1,0:T(8,128)}, u32[]{:S(2)}) copy-start(f32[5,135,135]{2,1,0:T(8,128)} %lower_hbm.1) | copy-start | bytes 1093504
  4.6 1.1 %copy-start.3 = (f32[5,135,135]{2,1,0:T(8,128)S(1)}, f32[5,135,135]{2,1,0:T(8,128)}, u32[]{:S(2)}) copy-start(f32[5,135,135]{2,1,0:T(8,128)} %upper_hbm.1) | copy-start | bytes 1093504
  5.7 0.9 %copy-start.4 = (f32[135,135]{1,0:T(8,128)S(1)}, f32[135,135]{1,0:T(8,128)}, u32[]{:S(2)}) copy-start(f32[135,135]{1,0:T(8,128)} %volume_hbm.1) | copy-start | bytes 218704
  6.6 0.8 %copy-start.5 = (f32[45,135]{1,0:T(8,128)S(1)}, f32[45,135]{1,0:T(8,128)}, u32[]{:S(2)}) copy-start(f32[45,135]{1,0:T(8,128)} %minus_hbm.1) | copy-start | bytes 72904
  7.4 0.8 %copy-start.6 = (f32[45,135]{1,0:T(8,128)S(1)}, f32[45,135]{1,0:T(8,128)}, u32[]{:S(2)}) copy-start(f32[45,135]{1,0:T(8,128)} %plus_hbm.1) | copy-start | bytes 72904
  8.2 0.8 %copy-start.7 = (f32[135,45]{0,1:T(8,128)S(1)}, f32[135,45]{0,1:T(8,128)}, u32[]{:S(2)}) copy-start(f32[135,45]{0,1:T(8,128)} %param.18) | copy-start | bytes 72904
  9.0 0.8 %copy-start.8 = (f32[135,45]{0,1:T(8,128)S(1)}, f32[135,45]{0,1:T(8,128)}, u32[]{:S(2)}) copy-start(f32[135,45]{0,1:T(8,128)} %param.19) | copy-start | bytes 72904

commit v3 on v2

--- a/solution.py
+++ b/solution.py
@@ -46,8 +46,8 @@
     lift_plus_hbm,
     offsets_hbm,
     counts_hbm,
-    out_state,
-    out_rate,
+    state_out,
+    rate_out,
     state,
     pivot_inv,
     lower_block,
@@ -60,6 +60,7 @@
     offsets,
     counts,
     load_sem,
+    store_sem,
     trace_m,
     lift_m,
     step_m,
@@ -334,19 +335,22 @@
     @pl.when(position == half - 1)
     def _():
         m_copy().wait_recv()
-        for c in range(chunks):
-            met = product(split(m_in[...]), y_out[c])
+        meets = [product(split(m_in[...]), y_out[c]) for c in range(chunks)]
+        starts = [
+            rows[0, :, columns[c]]
+            + product(take(reach_y, 0), y_in[c])
+            + product(take(reach_x, 0), meets[c])
+            for c in range(chunks)
+        ]
+        for c in range(chunks):
             x_copy(c).wait_recv()
-            x_in[c] = x_in[c] + met
 
             @pl.when(position > 0)
             def _():
-                x_out[c] = (
-                    rows[0, :, columns[c]]
-                    + product(take(reach_y, 0), y_in[c])
-                    + product(take(reach_x, 0), x_in[c])
-                )
+                x_out[c] = starts[c] + product(take(reach_x, 0), x_in[c])
                 x_copy(c).start()
+
+            x_in[c] = x_in[c] + meets[c]
 
     @pl.when(position > 0)
     def _():
@@ -370,10 +374,19 @@
             for k in range(elements):
                 rows[k, :, columns[c]] += product(take(reach_x, k), x_in[c])
 
+    def store(which, k):
+        return pltpu.make_async_copy(
+            (rows, state)[which].at[k],
+            (state_out, rate_out)[which].at[k],
+            store_sem.at[which, k],
+        )
+
     for k in range(elements):
-        out_state[k] = active(k) * rows[k]
-
-    start_rate(lambda k: out_state[k], 1)
+        rows[k] = active(k) * rows[k]
+
+    start_rate(lambda k: rows[k], 1)
+    for k in range(elements):
+        store(0, k).start()
 
     @pl.when(position < walls - 1)
     def _():
@@ -391,7 +404,11 @@
 
     wait_rate(1)
     for k in range(elements):
-        out_rate[k] = active(k) * rate(k, 1)
+        state[k] = active(k) * rate(k, 1)
+        store(1, k).start()
+    for which in range(2):
+        for k in range(elements):
+            store(which, k).wait()
 
 
 def solution(mesh):
@@ -416,7 +433,7 @@
         chunks = 2 if lines % 256 == 0 else 1
         width = lines // chunks
         halo_width = ceil_to(elements, 128)
-        vmem = pl.BlockSpec(memory_space=pltpu.VMEM)
+        hbm = pl.BlockSpec(memory_space=pltpu.HBM)
         operands = (
             state,
             pivot_inv,
@@ -433,11 +450,12 @@
         return pl.pallas_call(
             functools.partial(kernel, walls, streams),
             out_shape=(jax.ShapeDtypeStruct(state.shape, F32),) * 2,
-            in_specs=[pl.BlockSpec(memory_space=pltpu.HBM)] * 11,
-            out_specs=(vmem, vmem),
+            in_specs=[hbm] * 11,
+            out_specs=(hbm, hbm),
             scratch_shapes=[pltpu.VMEM(x.shape, x.dtype) for x in operands]
             + [
                 pltpu.SemaphoreType.DMA((len(operands),)),
+                pltpu.SemaphoreType.DMA((2, elements)),
                 pltpu.VMEM((2, size_pad + 2 * face_pad, size), BF16),
                 pltpu.VMEM((2, 2, size, face_pad), BF16),
                 pltpu.VMEM((2, elements, size, size), BF16),
@@ -467,7 +485,7 @@
                 pltpu.SemaphoreType.DMA,
             ],
             compiler_params=pltpu.CompilerParams(
-                collective_id=0, has_side_effects=True, vmem_limit_bytes=32 * 1024 * 1024
+                collective_id=0, has_side_effects=True, vmem_limit_bytes=67043328
             ),
         )(*operands)
 

time: 43.2 us -> 34.3 us (0.79)
  local copies, waits for them, and re-layouts: 10.9 us -> 2.92 us
  Pallas kernels: 31.1 us -> 30.6 us
    unnamed x24 -> x4, local copies, waits for them, and re-layouts: 10.9 us -> 2.92 us
    pallas_call x1, Pallas kernels: 31.1 us -> 30.6 us  [body(): pl.pallas_call(functools.partial(kernel, walls, streams), out_shape=(jax....]
where the time goes in v3:
time: 34.3 us; the launch traced here: 34.2 us
  Pallas kernels  30.6 us (89%)
  local copies, waits for them, and re-layouts  2.92 us (9%)
  between operations  0.65 us (2%)
    pallas_call x1, Pallas kernels, body(): pl.pallas_call(functools.partial(kernel, walls, streams), out_shape=(jax....  30.6 us
    unnamed x4, local copies, waits for them, and re-layouts  2.92 us

profile of v3, /device:TPU:1, one launch (start us, length us, event | category | flops | bytes accessed | tf_op | source)
XLA Modules:
  0.0 34.2 jit_solution(14489682093456299457)
XLA Ops:
  0.6 30.6 %shard_map.122 = (f32[5,135,256]{2,1,0:T(8,128)}, f32[5,135,256]{2,1,0:T(8,128)}) custom-call(f32[5,135,256]{2,1,0:T(8,128)} %state_hbm.1, f32[5,135,135]{2,1,0:T(8,128)} %pivot_hbm.1, f32[5,135,135]{2,1,0:T(8,128)} %lower_hbm.1, f32[5,135,135]{2,1,0:T(8,128)} %upper_hbm.1, f32[135,135]{1,0:T(8,128)} %volume_hbm.1, f32[45,135]{1,0:T(8,128)} %minus_hbm.1, ...), custom_call_target="tpu_custom_call" | custom-call | tf_op jit(solution)/shard_map/pallas_call | solution.py:450
  31.2 0.0 copy-start
  31.2 2.1 %copy.15 = f32[5,135,256]{2,1,0:T(8,128)} copy(f32[5,135,256]{2,1,0:T(8,128)} %get-tuple-element.4) | data formatting | bytes 1382400
  33.3 0.0 copy-done
  33.3 0.8 %copy.16 = f32[5,135,256]{2,1,0:T(8,128)} copy(f32[5,135,256]{2,1,0:T(8,128)S(1)} %copy-done) | data formatting | bytes 1382400
Async XLA Ops:
  31.2 2.1 %copy-start = (f32[5,135,256]{2,1,0:T(8,128)S(1)}, f32[5,135,256]{2,1,0:T(8,128)}, u32[]{:S(2)}) copy-start(f32[5,135,256]{2,1,0:T(8,128)} %get-tuple-element.5) | copy-start | bytes 2073604

commit v4 on v3

--- a/solution.py
+++ b/solution.py
@@ -77,6 +77,7 @@
     x_out,
     x_in,
     last,
+    exit_f,
     m_out,
     m_in,
     down_m,
@@ -223,18 +224,26 @@
         step = product(split(pivot_inv[k]), lower_block[k])
         put(step_m, k, step)
         put(upper_m, k, upper_block[k])
-    spikes = [-(step_m[0, 0].astype(F32) + step_m[1, 0].astype(F32))]
-    for k in range(1, elements):
-        spikes.append(-product(take(step_m, k), spikes[-1]))
-    put(exit_m, 0, spikes[-1])
-    map_y, map_x = spikes[-1], -upper_block[elements - 1]
-    put(reach_y, elements - 1, map_y)
-    put(reach_x, elements - 1, map_x)
-    for k in reversed(range(elements - 1)):
-        map_y = spikes[k] - product(take(upper_m, k), map_y)
-        map_x = -product(take(upper_m, k), map_x)
-        put(reach_y, k, map_y)
-        put(reach_x, k, map_x)
+
+    def form_spikes():
+        spike = -(step_m[0, 0].astype(F32) + step_m[1, 0].astype(F32))
+        put(reach_y, 0, spike)
+        for k in range(1, elements):
+            spike = -product(take(step_m, k), spike)
+            put(reach_y, k, spike)
+        exit_f[...] = spike
+        put(exit_m, 0, spike)
+
+    def form_reach():
+        map_y, map_x = exit_f[...], -upper_block[elements - 1]
+        put(reach_x, elements - 1, map_x)
+        for k in reversed(range(elements - 1)):
+            spike = reach_y[0, k].astype(F32) + reach_y[1, k].astype(F32)
+            map_y = spike - product(take(upper_m, k), map_y)
+            map_x = -product(take(upper_m, k), map_x)
+            put(reach_y, k, map_y)
+            put(reach_x, k, map_x)
+        return map_y
 
     def m_copy():
         return pltpu.make_async_remote_copy(
@@ -246,10 +255,15 @@
             device_id_type=MESH,
         )
 
-    @pl.when(position == walls - 1)
-    def _():
-        m_out[...] = map_y
-        m_copy().start()
+    @pl.when(position >= half)
+    def _():
+        form_spikes()
+        map_y = form_reach()
+
+        @pl.when(position == walls - 1)
+        def _():
+            m_out[...] = map_y
+            m_copy().start()
 
     wait_rate(0)
     local = None
@@ -288,6 +302,20 @@
             y_copy(c).start()
 
     last[...] = rows[elements - 1]
+
+    @pl.when(position < half)
+    def _():
+        form_spikes()
+
+    @pl.when(jnp.logical_and(position >= half, position < walls - 1))
+    def _():
+        m_copy().wait_recv()
+        put(down_m, 0, product(take(reach_x, 0), m_in[...]))
+        m_out[...] = (reach_y[0, 0].astype(F32) + reach_y[1, 0].astype(F32)) + product(
+            take(down_m, 0), exit_f[...]
+        )
+        m_copy().start()
+
     after = rows[elements - 1]
     for k in reversed(range(elements - 1)):
         after = rows[k] - product(take(upper_m, k), after)
@@ -301,13 +329,6 @@
 
     @pl.when(jnp.logical_and(position >= half, position < walls - 1))
     def _():
-        m_copy().wait_recv()
-        through = product(take(reach_x, 0), m_in[...])
-        put(down_m, 0, through)
-        m_out[...] = (reach_y[0, 0].astype(F32) + reach_y[1, 0].astype(F32)) + product(
-            take(down_m, 0), spikes[-1]
-        )
-        m_copy().start()
         above = rows[0] + product(take(down_m, 0), last[...])
         for c in range(chunks):
             x_copy(c).wait_recv()
@@ -320,6 +341,10 @@
             y_copy(c).wait_recv()
             y_out[c] = last[:, columns[c]] + product(take(exit_m, 0), y_in[c])
             y_copy(c).start()
+
+    @pl.when(position < half)
+    def _():
+        form_reach()
 
     @pl.when(position >= half)
     def _():
@@ -474,6 +499,7 @@
                 pltpu.VMEM((size, lines), F32),
                 pltpu.VMEM((size, size), F32),
                 pltpu.VMEM((size, size), F32),
+                pltpu.VMEM((size, size), F32),
                 pltpu.VMEM((2, 1, size, size), BF16),
                 pltpu.SemaphoreType.DMA((4,)),
                 pltpu.SemaphoreType.DMA((4,)),

time: 34.3 us -> 34.6 us (level)
  no operation moved by 1% of the time
where the time goes in v4:
time: 34.6 us; the launch traced here: 34.4 us
  Pallas kernels  30.8 us (89%)
  local copies, waits for them, and re-layouts  2.92 us (8%)
  between operations  0.65 us (2%)
    pallas_call x1, Pallas kernels, body(): pl.pallas_call(functools.partial(kernel, walls, streams), out_shape=(jax....  30.8 us
    unnamed x4, local copies, waits for them, and re-layouts  2.92 us

profile of v4, /device:TPU:1, one launch (start us, length us, event | category | flops | bytes accessed | tf_op | source)
XLA Modules:
  0.0 34.4 jit_solution(13533620964641880147)
XLA Ops:
  0.6 30.8 %shard_map.122 = (f32[5,135,256]{2,1,0:T(8,128)}, f32[5,135,256]{2,1,0:T(8,128)}) custom-call(f32[5,135,256]{2,1,0:T(8,128)} %state_hbm.1, f32[5,135,135]{2,1,0:T(8,128)} %pivot_hbm.1, f32[5,135,135]{2,1,0:T(8,128)} %lower_hbm.1, f32[5,135,135]{2,1,0:T(8,128)} %upper_hbm.1, f32[135,135]{1,0:T(8,128)} %volume_hbm.1, f32[45,135]{1,0:T(8,128)} %minus_hbm.1, ...), custom_call_target="tpu_custom_call" | custom-call | tf_op jit(solution)/shard_map/pallas_call | solution.py:475
  31.5 0.0 copy-start
  31.5 2.1 %copy.15 = f32[5,135,256]{2,1,0:T(8,128)} copy(f32[5,135,256]{2,1,0:T(8,128)} %get-tuple-element.4) | data formatting | bytes 1382400
  33.5 0.0 copy-done
  33.5 0.8 %copy.16 = f32[5,135,256]{2,1,0:T(8,128)} copy(f32[5,135,256]{2,1,0:T(8,128)S(1)} %copy-done) | data formatting | bytes 1382400
Async XLA Ops:
  31.5 2.1 %copy-start = (f32[5,135,256]{2,1,0:T(8,128)S(1)}, f32[5,135,256]{2,1,0:T(8,128)}, u32[]{:S(2)}) copy-start(f32[5,135,256]{2,1,0:T(8,128)} %get-tuple-element.5) | copy-start | bytes 2073604
